TPU v7x, 32 devices: a whole 2x2x4 slice. The times are simulated.
32 devices in a mesh: rep: 2 (over core), mp: 16 (over z, y, x).
Axes of the slice: x: 2, y: 2, z: 4, core: 2. Of those that a mesh axis runs over, the one named last changes fastest.
Arguments:
- lookup_block: int32 [2, 2048, 16, 4], P(None, ('rep', 'mp')), may hold values from 0 to 9
- lookup_offset: int32 [2, 2048, 16, 4], P(None, ('rep', 'mp')), may hold values from 0 to 63
- interaction_grad: bfloat16 [2, 2048, 16, 16], P(None, ('rep', 'mp')), may hold values from -4 to 4
- table: bfloat16 [49152, 256], P('mp'), may hold values from -0.3125 to 0.3125
- adagrad_state: float32 [49152], P('mp'), may hold values from 0.05 to 2
- touched_blocks: int32 [16, 10], P('mp'), may hold values from 0 to 47, as said below
- dither: int32 [16, 640, 256], P('mp'), may hold values from 0 to 32767
Outputs:
- new_table: bfloat16 [49152, 256], P('mp')
- new_state: float32 [49152], P('mp')
Inputs may be any that keep to these rules, and one draw needn't show every extreme that they name: `touched_blocks`: each row names 10 different row blocks.
All inputs are finite; a program needn't handle non-finite values.
Results may differ from a plain program's by a relative error of at most 0.00055.
The roundings to bfloat16 on the way count: a program that leaves them out, or rounds other values in their place, can miss the bound.
Values may be sent and summed in bfloat16 or wider, within the bound.
A program may use at most 128 MiB of HBM per device.

v0:
```python
import jax
import jax.numpy as jnp
from jax import lax
from jax.sharding import PartitionSpec as P

BLOCK = 64
LEARN_RATE = 0.1
POOL_DECAY = 0.5
DITHER_UNIT = 2.0 ** (-15)
SMALLEST = 2.0 ** (-14)


def dither_round(weights, dither_bits):
    magnitude = jnp.maximum(jnp.abs(weights), SMALLEST)
    spacing = jnp.exp2(jnp.floor(jnp.log2(magnitude)) - 7.0)
    grid_level = jnp.floor(weights / spacing + dither_bits.astype(jnp.float32) * DITHER_UNIT)
    return (grid_level * spacing).astype(jnp.bfloat16)


def adagrad_rows(slab_rows, grad_rows, state_rows, dither_bits):
    state_next = state_rows + jnp.mean(grad_rows * grad_rows, axis=-1)
    moved = (
        slab_rows.astype(jnp.float32)
        - LEARN_RATE * grad_rows / (jnp.sqrt(state_next) + 1e-08)[:, None]
    )
    return (dither_round(moved, dither_bits), state_next)


def hit_counts(lookup_rows, slab_size):
    column = lax.broadcasted_iota(jnp.int32, (1, slab_size), 1)
    counted = jnp.zeros((lookup_rows.shape[0], slab_size), jnp.bfloat16)
    for lookup in range(lookup_rows.shape[1]):
        counted = counted + (lookup_rows[:, lookup : lookup + 1] == column).astype(jnp.bfloat16)
    return counted


def pairwise(pooled_rows, cotangent):
    forward = jnp.einsum("bfg,bge->bfe", cotangent, pooled_rows, preferred_element_type=jnp.float32)
    backward = jnp.einsum(
        "bgf,bge->bfe", cotangent, pooled_rows, preferred_element_type=jnp.float32
    )
    return (forward + backward + POOL_DECAY * pooled_rows.astype(jnp.float32)).astype(jnp.bfloat16)


def per_device(
    lookup_block, lookup_offset, interaction_grad, table, adagrad_state, touched_blocks, dither
):
    micro_count, sample_count, feature_count, bag_count = lookup_block.shape
    groups = lax.axis_size("mp")
    row_count, emb_width = table.shape
    touch_count = touched_blocks.shape[1]
    slab_size = touch_count * BLOCK
    owner_samples = groups * sample_count
    lookup_rows = lookup_block * BLOCK + lookup_offset
    owner_rows = lax.all_to_all(lookup_rows, "mp", split_axis=2, concat_axis=1, tiled=True)
    owner_rows = owner_rows.reshape(micro_count, owner_samples, bag_count)
    table_blocks = table.reshape(row_count // BLOCK, BLOCK, emb_width)
    slab_table = table_blocks[touched_blocks[0]].reshape(slab_size, emb_width)
    counted = [hit_counts(owner_rows[micro_index], slab_size) for micro_index in range(micro_count)]
    pooled_rows = [
        jnp.dot(hits, slab_table, preferred_element_type=jnp.float32).astype(jnp.bfloat16)
        for hits in counted
    ]
    returned = []
    outgoing = jnp.stack(pooled_rows).reshape(micro_count, groups, sample_count, 1, emb_width)
    arrived = lax.all_to_all(outgoing, "mp", split_axis=1, concat_axis=3, tiled=True)
    sample_pooled = arrived.reshape(micro_count * sample_count, feature_count, emb_width)
    cot_rows = interaction_grad.reshape(micro_count * sample_count, feature_count, feature_count)
    grad_rows = pairwise(sample_pooled, cot_rows)
    grad_rows = grad_rows.reshape(micro_count, 1, sample_count, feature_count, emb_width)
    sent_back = lax.all_to_all(grad_rows, "mp", split_axis=3, concat_axis=1, tiled=True)
    sent_back = sent_back.reshape(micro_count, owner_samples, emb_width)
    returned = [sent_back[micro_index] for micro_index in range(micro_count)]
    slab_grad = jnp.zeros((slab_size, emb_width), jnp.float32)
    for micro_index in range(micro_count):
        slab_grad = slab_grad + jnp.einsum(
            "sr,se->re",
            counted[micro_index],
            returned[micro_index],
            preferred_element_type=jnp.float32,
        )
    state_slab = adagrad_state.reshape(row_count // BLOCK, BLOCK)[touched_blocks[0]].reshape(
        slab_size
    )
    summed_grad = lax.psum(slab_grad, "rep")
    new_rows, state_next = adagrad_rows(slab_table, summed_grad, state_slab, dither[0])
    updated_blocks = table_blocks.at[touched_blocks[0]].set(
        new_rows.reshape(touch_count, BLOCK, emb_width)
    )
    state_blocks = adagrad_state.reshape(row_count // BLOCK, BLOCK)
    updated_state = state_blocks.at[touched_blocks[0]].set(state_next.reshape(touch_count, BLOCK))
    return (updated_blocks.reshape(row_count, emb_width), updated_state.reshape(row_count))


def solution(mesh):
    return jax.shard_map(
        per_device,
        mesh=mesh,
        in_specs=(
            P(None, ("rep", "mp"), None, None),
            P(None, ("rep", "mp"), None, None),
            P(None, ("rep", "mp"), None, None),
            P("mp", None),
            P("mp"),
            P("mp", None),
            P("mp", None, None),
        ),
        out_specs=(P("mp", None), P("mp")),
        check_vma=False,
    )
```

profile of v0, /device:TPU:0, one launch (start us, length us, event | category | flops | bytes accessed | tf_op | source)
XLA Modules:
  0.0 124.7 jit_solution(17753280693400444190)
XLA Ops:
  7.2 1.5 %copy.46 = bf16[3072,256]{1,0:T(8,128)(2,1)S(1)} copy(bf16[3072,256]{1,0:T(8,128)(2,1)} %param.10) | data formatting | bytes 3145728
  8.7 0.7 reshape.142
  9.4 8.3 %all-to-all-start = ((s32[16,1,512]{2,1,0:T(1,128)}), s32[16,1,512]{2,1,0:T(1,128)S(1)}, u32[]{:S(2)}, u32[]{:S(2)}) async-start(s32[16,1,512]{2,1,0:T(1,128)} %reshape.142), calls=%async_computation | async-start | bytes 65536 | tf_op jit(solution)/shard_map/all_to_all | solution.py:55
  17.8 0.6 gather_fusion
  18.4 6.8 %all-to-all-done = s32[16,1,512]{2,1,0:T(1,128)S(1)} async-done(((s32[16,1,512]{2,1,0:T(1,128)}), s32[16,1,512]{2,1,0:T(1,128)S(1)}, u32[]{:S(2)}, u32[]{:S(2)}) %all-to-all-start) | async-done | bytes 32800 | tf_op jit(solution)/shard_map/all_to_all | solution.py:55
  25.2 0.5 broadcast.49
  25.7 0.7 reduce
  26.8 1.8 %convolution_convert_fusion.1 = bf16[1024,256]{1,0:T(8,128)(2,1)S(1)} fusion(bf16[640,256]{1,0:T(8,128)(2,1)S(1)} %bitcast.83, s32[1024]{0:T(1024)S(1)} %bitcast.91, s32[1024]{0:T(1024)S(1)} %bitcast.93, s32[1024]{0:T(1024)S(1)} %bitcast.95, s32[1024]{0:T(1024)S(1)} %bitcast.89), kind=kOutput, calls=%fused_computation.29 | convolution fusion | flops 346292224 | bytes 868352 | tf_op jit(solution)/shard_map/dot_general | solution.py:61
  28.6 1.8 %convolution_convert_fusion = bf16[1024,256]{1,0:T(8,128)(2,1)S(1)} fusion(bf16[640,256]{1,0:T(8,128)(2,1)S(1)} %bitcast.84, s32[1024]{0:T(1024)S(1)} %bitcast.99, s32[1024]{0:T(1024)S(1)} %bitcast.101, s32[1024]{0:T(1024)S(1)} %bitcast.103, s32[1024]{0:T(1024)S(1)} %bitcast.97), kind=kOutput, calls=%fused_computation.28 | convolution fusion | flops 346292224 | bytes 868352 | tf_op jit(solution)/shard_map/dot_general | solution.py:61
  30.3 1.1 pad_maximum_fusion
  31.4 3.7 %all-to-all-start.1 = ((bf16[2,16,64,1,256]{4,2,3,0,1:T(8,128)(2,1)}), bf16[2,16,64,1,256]{4,2,3,0,1:T(8,128)(2,1)S(1)}, u32[]{:S(2)}, u32[]{:S(2)}) async-start(bf16[2,16,64,1,256]{4,2,3,0,1:T(8,128)(2,1)} %pad_maximum_fusion), calls=%async_computation.1 | async-start | bytes 2097152 | tf_op jit(solution)/shard_map/all_to_all | solution.py:66
  35.1 1.4 %copy.30 = bf16[2,64,16,16]{2,3,1,0:T(8,128)(2,1)S(1)} copy(bf16[2,64,16,16]{1,3,2,0:T(8,128)(2,1)} %param.9) | data formatting | bytes 131072 | tf_op jit(solution)/shard_map/reshape | solution.py:68
  36.5 21.7 %all-to-all-done.1 = bf16[2,16,64,1,256]{4,2,3,0,1:T(8,128)(2,1)S(1)} async-done(((bf16[2,16,64,1,256]{4,2,3,0,1:T(8,128)(2,1)}), bf16[2,16,64,1,256]{4,2,3,0,1:T(8,128)(2,1)S(1)}, u32[]{:S(2)}, u32[]{:S(2)}) %all-to-all-start.1) | async-done | bytes 1048608 | tf_op jit(solution)/shard_map/all_to_all | solution.py:66
  58.3 0.6 copy.24
  60.2 30.6 %all_to_all.45 = bf16[2,1,64,16,256]{4,2,0,1,3:T(8,128)(2,1)S(1)} all-to-all(bf16[2,1,64,16,256]{4,2,0,1,3:T(8,128)(2,1)S(1)} %copy.28), channel_id=1, replica_groups=mesh['rep'=2,'mp'=16] {'mp'}, dimensions={3} | all-to-all | bytes 2097152 | tf_op jit(solution)/shard_map/all_to_all | solution.py:71
  91.0 1.7 %fusion.15 = f32[640,256]{1,0:T(8,128)S(1)} fusion(bf16[1024,256]{1,0:T(8,128)(2,1)S(1)} %bitcast.86, s32[1024]{0:T(1024)S(1)} %bitcast.92, s32[1024]{0:T(1024)S(1)} %bitcast.94, s32[1024]{0:T(1024)S(1)} %bitcast.96, s32[1024]{0:T(1024)S(1)} %bitcast.90), kind=kOutput, calls=%fused_computation.31 | convolution fusion | flops 346030080 | bytes 1196032 | tf_op jit(solution)/shard_map/sr,se->re/dot_general | solution.py:76
  92.8 2.5 %convolution_add_fusion = f32[640,256]{1,0:T(8,128)} fusion(f32[640,256]{1,0:T(8,128)S(1)} %fusion.15, bf16[1024,256]{1,0:T(8,128)(2,1)S(1)} %bitcast.85, s32[1024]{0:T(1024)S(1)} %bitcast.100, s32[1024]{0:T(1024)S(1)} %bitcast.102, s32[1024]{0:T(1024)S(1)} %bitcast.104, s32[1024]{0:T(1024)S(1)} %bitcast.98), kind=kOutput, calls=%fused_computation.30 | convolution fusion | flops 346193920 | bytes 1851392 | tf_op jit(solution)/shard_map/sr,se->re/dot_general | solution.py:76
  95.4 0.6 gather_fusion.1
  96.0 16.5 %all-reduce.2.cloned.1.call-done = f32[640,256]{1,0:T(8,128)} async-done(((f32[640,256]{1,0:T(8,128)}), f32[640,256]{1,0:T(8,128)}) %all-reduce.2.cloned.1.call-update) | async-done | bytes 655376 | tf_op jit(solution)/shard_map/psum | solution.py:85
  112.5 1.3 %multiply_reduce_fusion = f32[640]{0:T(1024)S(1)} fusion(f32[640,256]{1,0:T(8,128)} %all-reduce.2.cloned.1.call-done), kind=kLoop, calls=%fused_computation.38 | loop fusion | flops 327040 | bytes 657920 | tf_op jit(solution)/shard_map/reduce_sum | solution.py:21
  113.8 1.6 %fusion.22 = bf16[640,256]{1,0:T(8,128)(2,1)S(1)} fusion(s32[1,640,256]{2,1,0:T(8,128)S(1)} %copy-done.1, f32[640,256]{1,0:T(8,128)} %all-reduce.2.cloned.1.call-done, f32[640]{0:T(1024)S(1)} %get-tuple-element.15, bf16[10,64,256]{2,1,0:T(8,128)(2,1)S(1)} %gather_fusion), kind=kLoop, calls=%fused_computation.37 | loop fusion | flops 2785280 | bytes 1968640 | tf_op jit(solution)/shard_map/convert_element_type | solution.py:17
  115.4 1.0 scatter_fusion
  116.5 0.6 scatter_custom_fusion.1
  117.2 0.7 reshape.107
  (35 shorter events, 2.2 us)
Async XLA Ops:
  7.2 1.5 %copy-start.3 = (s32[2,64,16,4]{1,3,2,0:T(4,128)S(1)}, s32[2,64,16,4]{1,3,2,0:T(4,128)}, u32[]{:S(2)}) copy-start(s32[2,64,16,4]{1,3,2,0:T(4,128)} %param.7) | copy-start | bytes 98308
  7.2 1.5 %copy-start.2 = (s32[2,64,16,4]{1,3,2,0:T(4,128)S(1)}, s32[2,64,16,4]{1,3,2,0:T(4,128)}, u32[]{:S(2)}) copy-start(s32[2,64,16,4]{1,3,2,0:T(4,128)} %param.8) | copy-start | bytes 98308
  7.2 10.6 %copy-start.5 = (s32[1,10]{1,0:T(1,128)S(1)}, s32[1,10]{1,0:T(1,128)}, u32[]{:S(2)}) copy-start(s32[1,10]{1,0:T(1,128)} %param.12) | copy-start | bytes 124
  9.4 15.8 %all-to-all-start = ((s32[16,1,512]{2,1,0:T(1,128)}), s32[16,1,512]{2,1,0:T(1,128)S(1)}, u32[]{:S(2)}, u32[]{:S(2)}) async-start(s32[16,1,512]{2,1,0:T(1,128)} %reshape.142), calls=%async_computation | async-start | bytes 65536 | tf_op jit(solution)/shard_map/all_to_all | solution.py:55
  31.4 26.9 %all-to-all-start.1 = ((bf16[2,16,64,1,256]{4,2,3,0,1:T(8,128)(2,1)}), bf16[2,16,64,1,256]{4,2,3,0,1:T(8,128)(2,1)S(1)}, u32[]{:S(2)}, u32[]{:S(2)}) async-start(bf16[2,16,64,1,256]{4,2,3,0,1:T(8,128)(2,1)} %pad_maximum_fusion), calls=%async_computation.1 | async-start | bytes 2097152 | tf_op jit(solution)/shard_map/all_to_all | solution.py:66
  35.1 77.4 %all-reduce.2.cloned.1.call-start = ((), (), s32[]{:S(2)}) async-start(), calls=%async_computation.3 | async-start | bytes 1310720 | tf_op jit(solution)/shard_map/psum | solution.py:85
  92.7 2.5 %copy-start.4 = (f32[3072]{0:T(1024)S(1)}, f32[3072]{0:T(1024)}, u32[]{:S(2)}) copy-start(f32[3072]{0:T(1024)} %param.11) | copy-start | bytes 36868
  92.7 21.0 %copy-start.1 = (s32[1,640,256]{2,1,0:T(8,128)S(1)}, s32[1,640,256]{2,1,0:T(8,128)}, u32[]{:S(2)}) copy-start(s32[1,640,256]{2,1,0:T(8,128)} %param.13) | copy-start | bytes 1966084
  116.5 1.4 %copy-start = (bf16[48,64,256]{2,1,0:T(8,128)(2,1)}, bf16[48,64,256]{2,1,0:T(8,128)(2,1)S(1)}, u32[]{:S(2)}) copy-start(bf16[48,64,256]{2,1,0:T(8,128)(2,1)S(1)} %scatter_fusion) | copy-start | bytes 4718596
Sparse Core Ops, SparseCore 0:
  95.4 17.0 all-reduce.1
where the time goes:
time: 125 us
  waiting for transfers between devices  45 us (36%)
  blocking collectives  30.6 us (24%)
  between operations  14.3 us (11%)
  starting transfers between devices  12 us (10%)
  matrix products  8.71 us (7%)
  local copies, waits for them, and re-layouts  8.62 us (7%)
  other arithmetic  5.37 us (4%)
    all_to_all x1, blocking collectives, per_device(): lax.all_to_all(grad_rows, 'mp', split_axis=3, concat_axis=1, tiled=True)  30.6 us
    all_to_all x1, waiting for transfers between devices, per_device(): lax.all_to_all(outgoing, 'mp', split_axis=1, concat_axis=3, tiled=True)  21.7 us
    psum x1, waiting for transfers between devices, per_device(): summed_grad = lax.psum(slab_grad, 'rep')  16.5 us
    all_to_all x1, starting transfers between devices, per_device(): lax.all_to_all(lookup_rows, 'mp', split_axis=2, concat_axis=1, tiled=True)  8.34 us
    all_to_all x1, waiting for transfers between devices, per_device(): lax.all_to_all(lookup_rows, 'mp', split_axis=2, concat_axis=1, tiled=True)  6.79 us
    dot_general x2, matrix products, per_device(): jnp.einsum('sr,se->re', counted[micro_index], returned[micro_index], pref...  4.17 us
    all_to_all x1, starting transfers between devices, per_device(): lax.all_to_all(outgoing, 'mp', split_axis=1, concat_axis=3, tiled=True)  3.66 us
    dot_general x2, matrix products, per_device(): jnp.dot(hits, slab_table, preferred_element_type=jnp.float32)  3.58 us
  transfers between devices with their start and end apart: 3, of which 3 were waited for; matrix products, arithmetic and copies ran while one was open for 2% of the time, Pallas kernels for 0%

commit v1 on v0

--- a/solution.py
+++ b/solution.py
@@ -82,7 +82,7 @@
     state_slab = adagrad_state.reshape(row_count // BLOCK, BLOCK)[touched_blocks[0]].reshape(
         slab_size
     )
-    summed_grad = lax.psum(slab_grad, "rep")
+    summed_grad = jnp.sum(lax.all_gather(slab_grad, "rep"), axis=0)
     new_rows, state_next = adagrad_rows(slab_table, summed_grad, state_slab, dither[0])
     updated_blocks = table_blocks.at[touched_blocks[0]].set(
         new_rows.reshape(touch_count, BLOCK, emb_width)

time: 125 us -> 118 us (0.944)
  waiting for transfers between devices: 45 us -> 36 us
  other arithmetic: 5.37 us -> 6.95 us
    psum x1 -> x0, waiting for transfers between devices: 16.5 us -> none  [per_device(): summed_grad = lax.psum(slab_grad, 'rep')]
    all_gather x0 -> x1, waiting for transfers between devices: none -> 6.53 us  [per_device(): summed_grad = jnp.sum(lax.all_gather(slab_grad, 'rep'), axis=0)]
    reduce_sum x0 -> x1, other arithmetic: none -> 1.47 us  [per_device(): summed_grad = jnp.sum(lax.all_gather(slab_grad, 'rep'), axis=0)]
    scatter x1, other arithmetic: 0.63 us -> 1.92 us  [per_device(): state_blocks.at[touched_blocks[0]]]
    unnamed x15 -> x23, local copies, waits for them, and re-layouts: 2.3 us -> 3.27 us
  transfers between devices with their start and end apart: 3 -> 3, of which waited for: 3 -> 3; matrix products, arithmetic and copies ran while one was open for 2% -> 1% of each run, Pallas kernels for 0% -> 0%
where the time goes in v1:
time: 118 us; the launch traced here: 117 us
  waiting for transfers between devices  36 us (31%)
  blocking collectives  30.6 us (26%)
  between operations  14.3 us (12%)
  starting transfers between devices  12 us (10%)
  matrix products  8.69 us (7%)
  local copies, waits for them, and re-layouts  8.68 us (7%)
  other arithmetic  6.95 us (6%)
    all_to_all x1, blocking collectives, per_device(): lax.all_to_all(grad_rows, 'mp', split_axis=3, concat_axis=1, tiled=True)  30.6 us
    all_to_all x1, waiting for transfers between devices, per_device(): lax.all_to_all(outgoing, 'mp', split_axis=1, concat_axis=3, tiled=True)  22.7 us
    all_to_all x1, starting transfers between devices, per_device(): lax.all_to_all(lookup_rows, 'mp', split_axis=2, concat_axis=1, tiled=True)  8.34 us
    all_to_all x1, waiting for transfers between devices, per_device(): lax.all_to_all(lookup_rows, 'mp', split_axis=2, concat_axis=1, tiled=True)  6.78 us
    all_gather x1, waiting for transfers between devices, per_device(): summed_grad = jnp.sum(lax.all_gather(slab_grad, 'rep'), axis=0)  6.53 us
    dot_general x2, matrix products, per_device(): jnp.einsum('sr,se->re', counted[micro_index], returned[micro_index], pref...  4.16 us
    all_to_all x1, starting transfers between devices, per_device(): lax.all_to_all(outgoing, 'mp', split_axis=1, concat_axis=3, tiled=True)  3.66 us
    dot_general x2, matrix products, per_device(): jnp.dot(hits, slab_table, preferred_element_type=jnp.float32)  3.58 us
  transfers between devices with their start and end apart: 3, of which 3 were waited for; matrix products, arithmetic and copies ran while one was open for 1% of the time, Pallas kernels for 0%

profile of v1, /device:TPU:0, one launch (start us, length us, event | category | flops | bytes accessed | tf_op | source)
XLA Modules:
  0.0 117.3 jit_solution(5608396328332559606)
XLA Ops:
  7.2 1.5 %copy.45 = bf16[3072,256]{1,0:T(8,128)(2,1)S(1)} copy(bf16[3072,256]{1,0:T(8,128)(2,1)} %param.10) | data formatting | bytes 3145728
  8.7 0.7 reshape.146
  9.4 8.3 %all-to-all-start = ((s32[16,1,512]{2,1,0:T(1,128)}), s32[16,1,512]{2,1,0:T(1,128)S(1)}, u32[]{:S(2)}, u32[]{:S(2)}) async-start(s32[16,1,512]{2,1,0:T(1,128)} %reshape.146), calls=%async_computation | async-start | bytes 65536 | tf_op jit(solution)/shard_map/all_to_all | solution.py:55
  17.8 0.6 gather_fusion
  18.4 6.8 %all-to-all-done = s32[16,1,512]{2,1,0:T(1,128)S(1)} async-done(((s32[16,1,512]{2,1,0:T(1,128)}), s32[16,1,512]{2,1,0:T(1,128)S(1)}, u32[]{:S(2)}, u32[]{:S(2)}) %all-to-all-start) | async-done | bytes 32800 | tf_op jit(solution)/shard_map/all_to_all | solution.py:55
  25.2 0.5 broadcast.59
  25.7 0.7 reduce
  26.8 1.8 %convolution_convert_fusion.1 = bf16[1024,256]{1,0:T(8,128)(2,1)S(1)} fusion(bf16[640,256]{1,0:T(8,128)(2,1)S(1)} %bitcast.78, s32[1024]{0:T(1024)S(1)} %bitcast.86, s32[1024]{0:T(1024)S(1)} %bitcast.88, s32[1024]{0:T(1024)S(1)} %bitcast.90, s32[1024]{0:T(1024)S(1)} %bitcast.84), kind=kOutput, calls=%fused_computation.29 | convolution fusion | flops 346292224 | bytes 868352 | tf_op jit(solution)/shard_map/dot_general | solution.py:61
  28.6 1.8 %convolution_convert_fusion = bf16[1024,256]{1,0:T(8,128)(2,1)S(1)} fusion(bf16[640,256]{1,0:T(8,128)(2,1)S(1)} %bitcast.79, s32[1024]{0:T(1024)S(1)} %bitcast.94, s32[1024]{0:T(1024)S(1)} %bitcast.96, s32[1024]{0:T(1024)S(1)} %bitcast.98, s32[1024]{0:T(1024)S(1)} %bitcast.92), kind=kOutput, calls=%fused_computation.28 | convolution fusion | flops 346292224 | bytes 868352 | tf_op jit(solution)/shard_map/dot_general | solution.py:61
  30.4 1.1 pad_maximum_fusion
  31.4 3.7 %all-to-all-start.1 = ((bf16[2,16,64,1,256]{4,2,3,0,1:T(8,128)(2,1)}), bf16[2,16,64,1,256]{4,2,3,0,1:T(8,128)(2,1)S(1)}, u32[]{:S(2)}, u32[]{:S(2)}) async-start(bf16[2,16,64,1,256]{4,2,3,0,1:T(8,128)(2,1)} %pad_maximum_fusion), calls=%async_computation.1 | async-start | bytes 2097152 | tf_op jit(solution)/shard_map/all_to_all | solution.py:66
  35.6 22.7 %all-to-all-done.1 = bf16[2,16,64,1,256]{4,2,3,0,1:T(8,128)(2,1)S(1)} async-done(((bf16[2,16,64,1,256]{4,2,3,0,1:T(8,128)(2,1)}), bf16[2,16,64,1,256]{4,2,3,0,1:T(8,128)(2,1)S(1)}, u32[]{:S(2)}, u32[]{:S(2)}) %all-to-all-start.1) | async-done | bytes 1048608 | tf_op jit(solution)/shard_map/all_to_all | solution.py:66
  58.3 0.6 copy.24
  60.2 30.6 %all_to_all.45 = bf16[2,1,64,16,256]{4,2,0,1,3:T(8,128)(2,1)S(1)} all-to-all(bf16[2,1,64,16,256]{4,2,0,1,3:T(8,128)(2,1)S(1)} %copy.28), channel_id=1, replica_groups=mesh['rep'=2,'mp'=16] {'mp'}, dimensions={3} | all-to-all | bytes 2097152 | tf_op jit(solution)/shard_map/all_to_all | solution.py:71
  91.1 1.7 %fusion.15 = f32[640,256]{1,0:T(8,128)S(1)} fusion(bf16[1024,256]{1,0:T(8,128)(2,1)S(1)} %bitcast.81, s32[1024]{0:T(1024)S(1)} %bitcast.87, s32[1024]{0:T(1024)S(1)} %bitcast.89, s32[1024]{0:T(1024)S(1)} %bitcast.91, s32[1024]{0:T(1024)S(1)} %bitcast.85), kind=kOutput, calls=%fused_computation.31 | convolution fusion | flops 346030080 | bytes 1196032 | tf_op jit(solution)/shard_map/sr,se->re/dot_general | solution.py:76
  92.8 2.5 %convolution_add_fusion = f32[640,256]{1,0:T(8,128)} fusion(f32[640,256]{1,0:T(8,128)S(1)} %fusion.15, bf16[1024,256]{1,0:T(8,128)(2,1)S(1)} %bitcast.80, s32[1024]{0:T(1024)S(1)} %bitcast.95, s32[1024]{0:T(1024)S(1)} %bitcast.97, s32[1024]{0:T(1024)S(1)} %bitcast.99, s32[1024]{0:T(1024)S(1)} %bitcast.93), kind=kOutput, calls=%fused_computation.30 | convolution fusion | flops 346193920 | bytes 1851392 | tf_op jit(solution)/shard_map/sr,se->re/dot_general | solution.py:76
  95.4 0.6 copy-done.3
  96.0 0.6 gather_fusion.1
  96.6 6.5 %all-gather.3.cloned.1.call-done = f32[1280,256]{1,0:T(8,128)} async-done(((f32[640,256]{1,0:T(8,128)}), f32[1280,256]{1,0:T(8,128)}) %all-gather.3.cloned.1.call-update) | async-done | bytes 1310736 | tf_op jit(solution)/shard_map/all_gather | solution.py:85
  103.1 1.5 %reduce_sum.18 = f32[640,256]{1,0:T(8,128)S(1)} reduce(f32[2,640,256]{2,1,0:T(8,128)} %bitcast.77, f32[]{:T(128)} %constant.6.clone.1), dimensions={0}, to_apply=%region_0.0 | reduce | flops 163840 | bytes 1966084 | tf_op jit(solution)/shard_map/reduce_sum | solution.py:85
  104.9 1.9 %scatter_custom_fusion.1 = f32[48,64]{1,0:T(8,128)} fusion(f32[48,64]{1,0:T(8,128)} %copy-done.3, s32[10]{0:T(128)S(1)} %fusion.22, f32[10,64]{1,0:T(8,128)S(1)} %gather_fusion.1, f32[10,64]{1,0:T(8,128)S(1)} %div.23), kind=kCustom, calls=%fused_computation.42 | custom fusion | flops 640 | bytes 28672 | tf_op jit(solution)/shard_map/scatter | solution.py:91
  106.8 1.5 %multiply_convert_fusion = bf16[10,64,256]{2,1,0:T(8,128)(2,1)S(1)} fusion(f32[10,64,256]{2,1,0:T(8,128)S(1)} %bitcast.75, f32[10,64,256]{2,1,0:T(8,128)S(1)} %bitcast.76, bf16[10,64,256]{2,1,0:T(8,128)(2,1)} %copy-done.1, f32[10,64]{1,0:T(8,128)S(1)} %sqrt_add_fusion), kind=kLoop, calls=%fused_computation.34 | loop fusion | flops 2293760 | bytes 1968640 | tf_op jit(solution)/shard_map/convert_element_type | solution.py:17
  108.3 1.0 scatter_fusion
  109.3 0.8 reshape.110
  (45 shorter events, 3.2 us)
Async XLA Ops:
  7.2 1.5 %copy-start.7 = (s32[2,64,16,4]{1,3,2,0:T(4,128)S(1)}, s32[2,64,16,4]{1,3,2,0:T(4,128)}, u32[]{:S(2)}) copy-start(s32[2,64,16,4]{1,3,2,0:T(4,128)} %param.7) | copy-start | bytes 98308
  7.2 1.5 %copy-start.6 = (s32[2,64,16,4]{1,3,2,0:T(4,128)S(1)}, s32[2,64,16,4]{1,3,2,0:T(4,128)}, u32[]{:S(2)}) copy-start(s32[2,64,16,4]{1,3,2,0:T(4,128)} %param.8) | copy-start | bytes 98308
  7.2 10.6 %copy-start.9 = (s32[1,10]{1,0:T(1,128)S(1)}, s32[1,10]{1,0:T(1,128)}, u32[]{:S(2)}) copy-start(s32[1,10]{1,0:T(1,128)} %param.12) | copy-start | bytes 124
  9.4 15.8 %all-to-all-start = ((s32[16,1,512]{2,1,0:T(1,128)}), s32[16,1,512]{2,1,0:T(1,128)S(1)}, u32[]{:S(2)}, u32[]{:S(2)}) async-start(s32[16,1,512]{2,1,0:T(1,128)} %reshape.146), calls=%async_computation | async-start | bytes 65536 | tf_op jit(solution)/shard_map/all_to_all | solution.py:55
  18.4 10.2 %copy-start.1 = (bf16[10,64,256]{2,1,0:T(8,128)(2,1)}, bf16[10,64,256]{2,1,0:T(8,128)(2,1)S(1)}, u32[]{:S(2)}) copy-start(bf16[10,64,256]{2,1,0:T(8,128)(2,1)S(1)} %gather_fusion) | copy-start | bytes 983044
  30.4 4.8 %copy-start.5 = (bf16[2,64,16,16]{1,3,2,0:T(8,128)(2,1)S(1)}, bf16[2,64,16,16]{1,3,2,0:T(8,128)(2,1)}, u32[]{:S(2)}) copy-start(bf16[2,64,16,16]{1,3,2,0:T(8,128)(2,1)} %param.9) | copy-start | bytes 196612
  31.4 26.9 %all-to-all-start.1 = ((bf16[2,16,64,1,256]{4,2,3,0,1:T(8,128)(2,1)}), bf16[2,16,64,1,256]{4,2,3,0,1:T(8,128)(2,1)S(1)}, u32[]{:S(2)}, u32[]{:S(2)}) async-start(bf16[2,16,64,1,256]{4,2,3,0,1:T(8,128)(2,1)} %pad_maximum_fusion), calls=%async_computation.1 | async-start | bytes 2097152 | tf_op jit(solution)/shard_map/all_to_all | solution.py:66
  35.1 68.0 %all-gather.3.cloned.1.call-start = ((), (), s32[]{:S(2)}) async-start(), calls=%async_computation.3 | async-start | bytes 1966080 | tf_op jit(solution)/shard_map/all_gather | solution.py:85
  92.8 2.5 %copy-start.8 = (f32[3072]{0:T(1024)S(1)}, f32[3072]{0:T(1024)}, u32[]{:S(2)}) copy-start(f32[3072]{0:T(1024)} %param.11) | copy-start | bytes 36868
  92.8 3.8 %copy-start.2 = (s32[1,640,256]{2,1,0:T(8,128)S(1)}, s32[1,640,256]{2,1,0:T(8,128)}, u32[]{:S(2)}) copy-start(s32[1,640,256]{2,1,0:T(8,128)} %param.13) | copy-start | bytes 1966084
  95.4 0.6 copy-start.3
  106.8 2.5 %copy-start.4 = (f32[48,64]{1,0:T(8,128)S(1)}, f32[48,64]{1,0:T(8,128)}, u32[]{:S(2)}) copy-start(f32[48,64]{1,0:T(8,128)} %scatter_custom_fusion.1) | copy-start | bytes 36868
  109.3 1.1 copy-start
Sparse Core Ops, SparseCore 0:
  95.4 7.6 all-gather.2
